TPU v7x, 256 devices: a whole 4x4x8 slice. The times are simulated.
256 devices in a mesh: rows: 32 (over z_lo, x, core), sub: 8 (over y, z_hi).
Axes of the slice: x: 4, y: 4, z: 8 (z_hi: 2, z_lo: 4; z = z_hi * 4 + z_lo), core: 2. Of those that a mesh axis runs over, the one named last changes fastest.
Arguments:
- embeddings: bfloat16 [16384, 1024], P('rows', 'sub'), may hold values from -40 to 40
- rotation: bfloat16 [1024, 1024], P(None, 'sub'), may hold values from -0.1875 to 0.1875
- codebooks: float32 [64, 16, 256], P('sub'), may hold values from -6 to 6
Outputs:
- new_codebooks: float32 [64, 16, 256], P('sub')
- new_rotation: float32 [1024, 1024], P('rows', 'sub')
All inputs are finite; a program needn't handle non-finite values.
Results may differ from a plain program's by a relative error of at most 0.006.
The roundings to bfloat16 on the way count: a program that leaves them out, or rounds other values in their place, can miss the bound.
Values may be sent and summed in bfloat16 or wider, within the bound.
No kernel may reach another device: no remote copies, remote signals or barrier semaphores. Data moves between devices by JAX's collectives and lax.ppermute only.
A program may use at most 64 MiB of HBM per device.

v0:
```python
import jax
import jax.numpy as jnp
from jax import lax
from jax.sharding import PartitionSpec as P

SUB_DIM = 16
ITERS = 2
POLAR_ITER_COUNT = 2
softness_level = 4.0
prior_weight = 8.0
quintic_one = 3.4445
quintic_three = -4.775
quintic_five = 2.0315


def complete_feature_rows(embeddings):
    return lax.all_gather(embeddings, "sub", axis=1, tiled=True)


def subspace_pass(pieces, centroid_tables):
    books_low = centroid_tables.astype(jnp.bfloat16)

    def per_subspace(inputs):
        features, assignment_probs, codes_low = inputs
        cross_products = lax.dot_general(
            codes_low, features, (((0,), (0,)), ((), ())), preferred_element_type=jnp.float32
        )
        centroid_logits = (
            2.0 * cross_products - jnp.sum(assignment_probs * assignment_probs, axis=0)[:, None]
        ) / softness_level
        centroid_logits = centroid_logits - jnp.max(centroid_logits, axis=0, keepdims=True)
        exponent = jnp.exp(centroid_logits)
        weights = (exponent / jnp.sum(exponent, axis=0, keepdims=True)).astype(jnp.bfloat16)
        counts = jnp.sum(weights, axis=1, dtype=jnp.float32)
        totals = lax.dot_general(
            features, weights, (((1,), (1,)), ((), ())), preferred_element_type=jnp.float32
        )
        return (counts, totals, weights)

    return lax.map(per_subspace, (pieces, centroid_tables, books_low))


def per_device(embeddings, rotation, codebooks):
    row_count = embeddings.shape[0]
    width_own = rotation.shape[1]
    local_subs = codebooks.shape[0]
    full_x = complete_feature_rows(embeddings)
    rotated = lax.dot_general(
        rotation, full_x, (((0,), (1,)), ((), ())), preferred_element_type=jnp.float32
    ).astype(jnp.bfloat16)
    pieces = rotated.reshape(local_subs, SUB_DIM, row_count)
    books_now = codebooks
    weights = None
    for repeat in range(ITERS):
        counts, totals, weights = subspace_pass(pieces, books_now)
        totals, counts = lax.psum((totals, counts), "rows")
        books_now = (totals + prior_weight * books_now) / (counts[:, None, :] + prior_weight)
    books_low = books_now.astype(jnp.bfloat16)
    rebuilt = jnp.einsum("mdk,mkr->mdr", books_low, weights, preferred_element_type=jnp.float32)
    rebuilt = rebuilt.reshape(width_own, row_count).astype(jnp.bfloat16)
    row_share = full_x.shape[1] // lax.axis_size("rows")
    partial_value = lax.dot_general(
        full_x, rebuilt, (((0,), (1,)), ((), ())), preferred_element_type=jnp.float32
    )
    summed = lax.psum(partial_value, "rows")
    own_cross = lax.dynamic_slice_in_dim(summed, lax.axis_index("rows") * row_share, row_share, 0)
    frob_norm = jnp.sqrt(lax.psum(jnp.sum(own_cross * own_cross), ("rows", "sub")) + 1e-06)
    polar_now = own_cross / frob_norm
    for polar_rotation_step in range(POLAR_ITER_COUNT):
        columns = lax.all_gather(polar_now, "rows", axis=0, tiled=True)
        gram_part = lax.dot_general(
            polar_now,
            columns,
            (((1,), (1,)), ((), ())),
            precision=lax.Precision.HIGHEST,
            preferred_element_type=jnp.float32,
        )
        gram_rows = lax.psum(gram_part, "sub")
        image = jnp.dot(
            gram_rows, columns, precision=lax.Precision.HIGHEST, preferred_element_type=jnp.float32
        )
        image_cols = lax.all_gather(image, "rows", axis=0, tiled=True)
        second = jnp.dot(
            gram_rows,
            image_cols,
            precision=lax.Precision.HIGHEST,
            preferred_element_type=jnp.float32,
        )
        polar_now = quintic_one * polar_now + quintic_three * image + quintic_five * second
    return (books_now, polar_now)


def solution(mesh):
    return jax.shard_map(
        per_device,
        mesh=mesh,
        in_specs=(P("rows", "sub"), P(None, "sub"), P("sub", None, None)),
        out_specs=(P("sub", None, None), P("rows", "sub")),
        check_vma=False,
    )
```

profile of v0, /device:TPU:1, one launch (start us, length us, event | category | flops | bytes accessed | tf_op | source)
XLA Modules:
  0.0 1482.6 jit_solution(5863832114635413068)
XLA Ops:
  7.2 0.7 all-gather.2.cloned.1.call-update
  8.0 0.9 convert_element_type.30
  8.9 65.7 %all-gather.2.cloned.1.call-done = bf16[512,1024]{1,0:T(8,128)(2,1)} async-done(((bf16[512,128]{1,0:T(8,128)(2,1)}), bf16[512,1024]{1,0:T(8,128)(2,1)}) %all-gather.2.cloned.1.call-update) | async-done | bytes 1048592 | tf_op jit(solution)/shard_map/all_gather | solution.py:17
  74.6 1.7 convolution_convert_fusion.1
  76.4 12.3 while.26
  76.4 0.7 multiply_reduce_fusion.5
  77.1 0.3 fusion.65
  77.9 0.7 multiply_reduce_fusion.5
  78.7 0.3 fusion.65
  79.5 0.7 multiply_reduce_fusion.5
  80.2 0.3 fusion.65
  81.0 0.7 multiply_reduce_fusion.5
  81.7 0.3 fusion.65
  82.5 0.7 multiply_reduce_fusion.5
  83.3 0.3 fusion.65
  84.1 0.7 multiply_reduce_fusion.5
  84.8 0.3 fusion.65
  85.6 0.7 multiply_reduce_fusion.5
  86.3 0.3 fusion.65
  87.1 0.7 multiply_reduce_fusion.5
  87.9 0.3 fusion.65
  88.7 69.8 %psum.57 = f32[8,256]{1,0:T(8,128)S(1)} all-reduce(f32[8,256]{1,0:T(8,128)S(1)} %get-tuple-element.75), channel_id=1, replica_groups=mesh['rows'=32,'sub'=8] {'rows'}, use_global_device_ids=true, to_apply=%region_7.8 | all-reduce | flops 2048 | bytes 16384 | tf_op jit(solution)/shard_map/psum | solution.py:56
  158.6 247.6 %all-reduce.6.cloned.1.call-done = f32[8,16,256]{2,1,0:T(8,128)} async-done(((f32[8,16,256]{2,1,0:T(8,128)}), f32[8,16,256]{2,1,0:T(8,128)}) %all-reduce.6.cloned.1.call-update) | async-done | bytes 131088 | tf_op jit(solution)/shard_map/psum | solution.py:56
  406.1 1.0 fusion.27
  407.1 0.7 broadcast.46
  407.8 11.8 while.27
  407.8 0.3 fusion.70
  408.3 0.8 fusion.72
  409.3 0.3 fusion.70
  409.8 0.8 fusion.72
  410.8 0.3 fusion.70
  411.3 0.8 fusion.72
  412.3 0.3 fusion.70
  412.7 0.8 fusion.72
  413.7 0.3 fusion.70
  414.2 0.8 fusion.72
  415.2 0.3 fusion.70
  415.7 0.8 fusion.72
  416.7 0.3 fusion.70
  417.2 0.8 fusion.72
  418.2 0.3 fusion.70
  418.7 0.8 fusion.72
  419.6 70.0 %psum.59 = f32[8,256]{1,0:T(8,128)S(1)} all-reduce(f32[8,256]{1,0:T(8,128)S(1)} %get-tuple-element.77), channel_id=1, replica_groups=mesh['rows'=32,'sub'=8] {'rows'}, use_global_device_ids=true, to_apply=%region_15.16 | all-reduce | flops 2048 | bytes 16384 | tf_op jit(solution)/shard_map/psum | solution.py:56
  489.7 252.1 %all-reduce.8.cloned.1.call-done = f32[8,16,256]{2,1,0:T(8,128)} async-done(((f32[8,16,256]{2,1,0:T(8,128)}), f32[8,16,256]{2,1,0:T(8,128)}) %all-reduce.8.cloned.1.call-update) | async-done | bytes 131088 | tf_op jit(solution)/shard_map/psum | solution.py:56
  741.8 0.9 add_divide_fusion
  742.7 0.4 convolution_convert_fusion
  743.1 0.3 copy-done.2
  743.4 1.4 convolution_bitcast_fusion.2
  744.8 275.9 %all-reduce.10.cloned.1.call-done = f32[1024,128]{1,0:T(8,128)} async-done(((f32[1024,128]{1,0:T(8,128)}), f32[1024,128]{1,0:T(8,128)}) %all-reduce.10.cloned.1.call-update) | async-done | bytes 524304 | tf_op jit(solution)/shard_map/psum | solution.py:65
  1020.8 1.3 multiply_reduce_fusion.2
  1022.1 78.1 %psum.61 = f32[]{:T(128)} all-reduce(f32[]{:T(128)} %multiply_reduce_fusion.2), channel_id=1, replica_groups=mesh['rows'=32,'sub'=8] {'rows','sub'}, use_global_device_ids=true, to_apply=%region_18.19 | all-reduce | flops 1 | bytes 8 | tf_op jit(solution)/shard_map/psum | solution.py:67
  1100.8 0.7 dynamic-slice_divide_fusion
  1101.6 39.9 %all_gather.16 = f32[1024,128]{1,0:T(8,128)S(1)} all-gather(f32[32,128]{1,0:T(8,128)S(1)} %dynamic-slice_divide_fusion), channel_id=1, replica_groups=mesh['rows'=32,'sub'=8] {'rows'}, dimensions={0}, use_global_device_ids=true | all-gather | bytes 540672 | tf_op jit(solution)/shard_map/all_gather | solution.py:70
  1141.5 1.3 fusion.30
  1142.8 95.5 %all-reduce.12.cloned.1.call-done = f32[32,1024]{1,0:T(8,128)} async-done(((f32[32,1024]{1,0:T(8,128)}), f32[32,1024]{1,0:T(8,128)}) %all-reduce.12.cloned.1.call-update) | async-done | bytes 131088 | tf_op jit(solution)/shard_map/psum | solution.py:78
  1238.3 1.3 fusion.31
  1239.6 47.8 %all_gather.17 = f32[1024,128]{1,0:T(8,128)S(1)} all-gather(f32[32,128]{1,0:T(8,128)S(1)} %fusion.31), channel_id=1, replica_groups=mesh['rows'=32,'sub'=8] {'rows'}, dimensions={0}, use_global_device_ids=true | all-gather | bytes 540672 | tf_op jit(solution)/shard_map/all_gather | solution.py:82
  1287.5 1.3 fusion.25
  1288.8 39.3 %all_gather.18 = f32[1024,128]{1,0:T(8,128)S(1)} all-gather(f32[32,128]{1,0:T(8,128)S(1)} %fusion.25), channel_id=1, replica_groups=mesh['rows'=32,'sub'=8] {'rows'}, dimensions={0}, use_global_device_ids=true | all-gather | bytes 540672 | tf_op jit(solution)/shard_map/all_gather | solution.py:70
  1328.1 1.3 fusion.32
  1329.3 95.4 %all-reduce.14.cloned.1.call-done = f32[32,1024]{1,0:T(8,128)} async-done(((f32[32,1024]{1,0:T(8,128)}), f32[32,1024]{1,0:T(8,128)}) %all-reduce.14.cloned.1.call-update) | async-done | bytes 131088 | tf_op jit(solution)/shard_map/psum | solution.py:78
  1424.7 1.3 fusion.33
  1426.0 47.8 %all_gather.19 = f32[1024,128]{1,0:T(8,128)S(1)} all-gather(f32[32,128]{1,0:T(8,128)S(1)} %fusion.33), channel_id=1, replica_groups=mesh['rows'=32,'sub'=8] {'rows'}, dimensions={0}, use_global_device_ids=true | all-gather | bytes 540672 | tf_op jit(solution)/shard_map/all_gather | solution.py:82
  1473.9 1.9 fusion.24
  (96 shorter events, 7.4 us)
Async XLA Ops:
  7.2 67.5 %copy-start = (bf16[1024,128]{1,0:T(8,128)(2,1)S(1)}, bf16[1024,128]{1,0:T(8,128)(2,1)}, u32[]{:S(2)}) copy-start(bf16[1024,128]{1,0:T(8,128)(2,1)} %param.8) | copy-start | bytes 786436
  7.2 67.5 %all-gather.2.cloned.1.call-start = ((), (), s32[]{:S(2)}) async-start(), calls=%async_computation | async-start | bytes 1179648 | tf_op jit(solution)/shard_map/all_gather | solution.py:17
  7.9 398.2 %all-reduce.6.cloned.1.call-start = ((), (), s32[]{:S(2)}) async-start(), calls=%async_computation.1 | async-start | bytes 262144 | tf_op jit(solution)/shard_map/psum | solution.py:56
  88.7 69.8 %copy-start.3 = (f32[8,16,256]{2,1,0:T(8,128)}, f32[8,16,256]{2,1,0:T(8,128)S(1)}, u32[]{:S(2)}) copy-start(f32[8,16,256]{2,1,0:T(8,128)S(1)} %get-tuple-element.74) | copy-start | bytes 393220
  158.5 583.3 %all-reduce.8.cloned.1.call-start = ((), (), s32[]{:S(2)}) async-start(), calls=%async_computation.2 | async-start | bytes 262144 | tf_op jit(solution)/shard_map/psum | solution.py:56
  419.6 323.8 %copy-start.1 = (bf16[512,1024]{1,0:T(8,128)(2,1)S(1)}, bf16[512,1024]{1,0:T(8,128)(2,1)}, u32[]{:S(2)}) copy-start(bf16[512,1024]{1,0:T(8,128)(2,1)} %all-gather.2.cloned.1.call-done) | copy-start | bytes 3145732
  489.7 531.1 %all-reduce.10.cloned.1.call-start = ((), (), s32[]{:S(2)}) async-start(), calls=%async_computation.3 | async-start | bytes 1048576 | tf_op jit(solution)/shard_map/psum | solution.py:65
  742.7 0.7 copy-start.2
  744.8 493.5 %all-reduce.12.cloned.1.call-start = ((), (), s32[]{:S(2)}) async-start(), calls=%async_computation.4 | async-start | bytes 262144 | tf_op jit(solution)/shard_map/psum | solution.py:78
  1142.8 282.0 %all-reduce.14.cloned.1.call-start = ((), (), s32[]{:S(2)}) async-start(), calls=%async_computation.5 | async-start | bytes 262144 | tf_op jit(solution)/shard_map/psum | solution.py:78
Sparse Core Ops, SparseCore 0:
  10.5 64.1 all-gather.1
  158.6 247.4 all-reduce.5
  489.8 251.9 all-reduce.7
  744.9 275.8 all-reduce.9
  1142.9 95.3 all-reduce.11
  1329.5 95.2 all-reduce.13
where the time goes:
time: 1480 us
  waiting for transfers between devices  1030 us (70%)
  blocking collectives  393 us (27%)
  matrix products  23.6 us (2%)
  other arithmetic  15.8 us (1%)
  between operations  15 us (1%)
    psum x2, waiting for transfers between devices, per_device(): totals, counts = lax.psum((totals, counts), 'rows')  500 us
    psum x1, waiting for transfers between devices, per_device(): summed = lax.psum(partial_value, 'rows')  276 us
    psum x2, waiting for transfers between devices, per_device(): gram_rows = lax.psum(gram_part, 'sub')  191 us
    psum x2, blocking collectives, per_device(): totals, counts = lax.psum((totals, counts), 'rows')  140 us
    all_gather x2, blocking collectives, per_device(): image_cols = lax.all_gather(image, 'rows', axis=0, tiled=True)  95.7 us
    all_gather x2, blocking collectives, per_device(): columns = lax.all_gather(polar_now, 'rows', axis=0, tiled=True)  79.2 us
    psum x1, blocking collectives, per_device(): lax.psum(jnp.sum(own_cross * own_cross), ('rows', 'sub')) + 1e-06  78.1 us
    all_gather x1, waiting for transfers between devices, complete_feature_rows(): return lax.all_gather(embeddings, 'sub', axis=1, tiled=True)  65.7 us
  transfers between devices with their start and end apart: 6, of which 6 were waited for; matrix products, arithmetic and copies ran while one was open for 0% of the time, Pallas kernels for 0%

commit v1 on v0

--- a/solution.py
+++ b/solution.py
@@ -62,7 +62,7 @@
     partial_value = lax.dot_general(
         full_x, rebuilt, (((0,), (1,)), ((), ())), preferred_element_type=jnp.float32
     )
-    summed = lax.psum(partial_value, "rows")
+    summed = jnp.sum(lax.all_gather(partial_value, "rows"), axis=0)
     own_cross = lax.dynamic_slice_in_dim(summed, lax.axis_index("rows") * row_share, row_share, 0)
     frob_norm = jnp.sqrt(lax.psum(jnp.sum(own_cross * own_cross), ("rows", "sub")) + 1e-06)
     polar_now = own_cross / frob_norm

time: 1480 us -> 1330 us (0.90)
  waiting for transfers between devices: 1030 us -> 856 us
  local copies, waits for them, and re-layouts: 1.74 us -> 19.6 us
    psum x1 -> x0, waiting for transfers between devices: 276 us -> none  [per_device(): summed = lax.psum(partial_value, 'rows')]
    all_gather x0 -> x1, waiting for transfers between devices: none -> 100 us  [per_device(): summed = jnp.sum(lax.all_gather(partial_value, 'rows'), axis=0)]
    unnamed x8 -> x10, local copies, waits for them, and re-layouts: 0.3 us -> 18 us
where the time goes in v1:
time: 1330 us
  waiting for transfers between devices  856 us (64%)
  blocking collectives  395 us (30%)
  other arithmetic  23.4 us (2%)
  matrix products  23.4 us (2%)
  local copies, waits for them, and re-layouts  19.6 us (1%)
  between operations  15 us (1%)
    psum x2, waiting for transfers between devices, per_device(): totals, counts = lax.psum((totals, counts), 'rows')  500 us
    psum x2, waiting for transfers between devices, per_device(): gram_rows = lax.psum(gram_part, 'sub')  189 us
    psum x2, blocking collectives, per_device(): totals, counts = lax.psum((totals, counts), 'rows')  140 us
    all_gather x1, waiting for transfers between devices, per_device(): summed = jnp.sum(lax.all_gather(partial_value, 'rows'), axis=0)  100 us
    all_gather x2, blocking collectives, per_device(): image_cols = lax.all_gather(image, 'rows', axis=0, tiled=True)  95.9 us
    all_gather x2, blocking collectives, per_device(): columns = lax.all_gather(polar_now, 'rows', axis=0, tiled=True)  81.7 us
    psum x1, blocking collectives, per_device(): lax.psum(jnp.sum(own_cross * own_cross), ('rows', 'sub')) + 1e-06  77.5 us
    all_gather x1, waiting for transfers between devices, complete_feature_rows(): return lax.all_gather(embeddings, 'sub', axis=1, tiled=True)  65.7 us
  transfers between devices with their start and end apart: 6, of which 6 were waited for; matrix products, arithmetic and copies ran while one was open for 0% of the time, Pallas kernels for 0%

profile of v1, /device:TPU:1, one launch (start us, length us, event | category | flops | bytes accessed | tf_op | source)
XLA Modules:
  0.0 1332.5 jit_solution(9058181554135349185)
XLA Ops:
  7.2 0.7 all-gather.4.cloned.1.call-update
  8.0 0.9 convert_element_type.30
  8.9 65.7 %all-gather.4.cloned.1.call-done = bf16[512,1024]{1,0:T(8,128)(2,1)} async-done(((bf16[512,128]{1,0:T(8,128)(2,1)}), bf16[512,1024]{1,0:T(8,128)(2,1)}) %all-gather.4.cloned.1.call-update) | async-done | bytes 1048592 | tf_op jit(solution)/shard_map/all_gather | solution.py:17
  74.6 1.7 convolution_convert_fusion.1
  76.4 12.3 while.26
  76.4 0.7 multiply_reduce_fusion.5
  77.1 0.3 fusion.65
  77.9 0.7 multiply_reduce_fusion.5
  78.7 0.3 fusion.65
  79.5 0.7 multiply_reduce_fusion.5
  80.2 0.3 fusion.65
  81.0 0.7 multiply_reduce_fusion.5
  81.8 0.3 fusion.65
  82.5 0.7 multiply_reduce_fusion.5
  83.3 0.3 fusion.65
  84.1 0.7 multiply_reduce_fusion.5
  84.8 0.3 fusion.65
  85.6 0.7 multiply_reduce_fusion.5
  86.4 0.3 fusion.65
  87.2 0.7 multiply_reduce_fusion.5
  87.9 0.3 fusion.65
  88.7 69.7 %psum.50 = f32[8,256]{1,0:T(8,128)S(1)} all-reduce(f32[8,256]{1,0:T(8,128)S(1)} %get-tuple-element.75), channel_id=1, replica_groups=mesh['rows'=32,'sub'=8] {'rows'}, use_global_device_ids=true, to_apply=%region_7.8 | all-reduce | flops 2048 | bytes 16384 | tf_op jit(solution)/shard_map/psum | solution.py:56
  158.5 247.6 %all-reduce.5.cloned.1.call-done = f32[8,16,256]{2,1,0:T(8,128)} async-done(((f32[8,16,256]{2,1,0:T(8,128)}), f32[8,16,256]{2,1,0:T(8,128)}) %all-reduce.5.cloned.1.call-update) | async-done | bytes 131088 | tf_op jit(solution)/shard_map/psum | solution.py:56
  406.1 1.0 fusion.27
  407.1 0.7 broadcast.46
  407.8 11.8 while.27
  408.3 0.8 fusion.72
  409.3 0.3 fusion.70
  409.8 0.8 fusion.72
  410.8 0.3 fusion.70
  411.3 0.8 fusion.72
  412.3 0.3 fusion.70
  412.7 0.8 fusion.72
  413.7 0.3 fusion.70
  414.2 0.8 fusion.72
  415.2 0.3 fusion.70
  415.7 0.8 fusion.72
  416.7 0.3 fusion.70
  417.2 0.8 fusion.72
  418.2 0.3 fusion.70
  418.7 0.8 fusion.72
  419.7 70.0 %psum.52 = f32[8,256]{1,0:T(8,128)S(1)} all-reduce(f32[8,256]{1,0:T(8,128)S(1)} %get-tuple-element.77), channel_id=1, replica_groups=mesh['rows'=32,'sub'=8] {'rows'}, use_global_device_ids=true, to_apply=%region_15.16 | all-reduce | flops 2048 | bytes 16384 | tf_op jit(solution)/shard_map/psum | solution.py:56
  489.7 252.1 %all-reduce.7.cloned.1.call-done = f32[8,16,256]{2,1,0:T(8,128)} async-done(((f32[8,16,256]{2,1,0:T(8,128)}), f32[8,16,256]{2,1,0:T(8,128)}) %all-reduce.7.cloned.1.call-update) | async-done | bytes 131088 | tf_op jit(solution)/shard_map/psum | solution.py:56
  741.8 0.9 add_divide_fusion
  742.8 0.4 convolution_convert_fusion
  743.1 0.3 copy-done.2
  743.4 1.1 convolution_bitcast_fusion.2
  744.6 100.3 %all-gather.6.cloned.1.call-done = f32[32768,128]{0,1:T(8,128)} async-done(((f32[1024,128]{0,1:T(8,128)}), f32[32768,128]{0,1:T(8,128)}) %all-gather.6.cloned.1.call-update) | async-done | bytes 16777232 | tf_op jit(solution)/shard_map/all_gather | solution.py:65
  844.9 17.7 %copy.7 = f32[16,8,32,1024]{3,2,1,0:T(8,128)} copy(f32[16,8,32,1024]{3,1,2,0:T(8,128)} %bitcast.90) | data formatting | bytes 33554432
  862.6 9.0 bitcast_reduce_fusion
  871.8 0.6 multiply_reduce_fusion.2
  872.4 77.5 %psum.53 = f32[]{:T(128)} all-reduce(f32[]{:T(128)} %multiply_reduce_fusion.2), channel_id=1, replica_groups=mesh['rows'=32,'sub'=8] {'rows','sub'}, use_global_device_ids=true, to_apply=%region_18.19 | all-reduce | flops 1 | bytes 8 | tf_op jit(solution)/shard_map/psum | solution.py:67
  950.6 42.4 %all_gather.24 = f32[1024,128]{1,0:T(8,128)S(1)} all-gather(f32[32,128]{1,0:T(8,128)S(1)} %broadcast_divide_fusion), channel_id=1, replica_groups=mesh['rows'=32,'sub'=8] {'rows'}, dimensions={0}, use_global_device_ids=true | all-gather | bytes 540672 | tf_op jit(solution)/shard_map/all_gather | solution.py:70
  993.0 1.3 fusion.30
  994.3 93.6 %all-reduce.9.cloned.1.call-done = f32[32,1024]{1,0:T(8,128)} async-done(((f32[32,1024]{1,0:T(8,128)}), f32[32,1024]{1,0:T(8,128)}) %all-reduce.9.cloned.1.call-update) | async-done | bytes 131088 | tf_op jit(solution)/shard_map/psum | solution.py:78
  1088.0 1.3 fusion.31
  1089.3 48.0 %all_gather.25 = f32[1024,128]{1,0:T(8,128)S(1)} all-gather(f32[32,128]{1,0:T(8,128)S(1)} %fusion.31), channel_id=1, replica_groups=mesh['rows'=32,'sub'=8] {'rows'}, dimensions={0}, use_global_device_ids=true | all-gather | bytes 540672 | tf_op jit(solution)/shard_map/all_gather | solution.py:82
  1137.3 1.3 fusion.25
  1138.6 39.3 %all_gather.26 = f32[1024,128]{1,0:T(8,128)S(1)} all-gather(f32[32,128]{1,0:T(8,128)S(1)} %fusion.25), channel_id=1, replica_groups=mesh['rows'=32,'sub'=8] {'rows'}, dimensions={0}, use_global_device_ids=true | all-gather | bytes 540672 | tf_op jit(solution)/shard_map/all_gather | solution.py:70
  1177.9 1.3 fusion.32
  1179.2 95.4 %all-reduce.11.cloned.1.call-done = f32[32,1024]{1,0:T(8,128)} async-done(((f32[32,1024]{1,0:T(8,128)}), f32[32,1024]{1,0:T(8,128)}) %all-reduce.11.cloned.1.call-update) | async-done | bytes 131088 | tf_op jit(solution)/shard_map/psum | solution.py:78
  1274.6 1.3 fusion.33
  1275.9 47.8 %all_gather.27 = f32[1024,128]{1,0:T(8,128)S(1)} all-gather(f32[32,128]{1,0:T(8,128)S(1)} %fusion.33), channel_id=1, replica_groups=mesh['rows'=32,'sub'=8] {'rows'}, dimensions={0}, use_global_device_ids=true | all-gather | bytes 540672 | tf_op jit(solution)/shard_map/all_gather | solution.py:82
  1323.7 1.9 fusion.24
  (100 shorter events, 7.8 us)
Async XLA Ops:
  7.2 67.5 %copy-start = (bf16[1024,128]{1,0:T(8,128)(2,1)S(1)}, bf16[1024,128]{1,0:T(8,128)(2,1)}, u32[]{:S(2)}) copy-start(bf16[1024,128]{1,0:T(8,128)(2,1)} %param.8) | copy-start | bytes 786436
  7.2 67.5 %all-gather.4.cloned.1.call-start = ((), (), s32[]{:S(2)}) async-start(), calls=%async_computation | async-start | bytes 1179648 | tf_op jit(solution)/shard_map/all_gather | solution.py:17
  7.9 398.2 %all-reduce.5.cloned.1.call-start = ((), (), s32[]{:S(2)}) async-start(), calls=%async_computation.1 | async-start | bytes 262144 | tf_op jit(solution)/shard_map/psum | solution.py:56
  88.7 69.7 %copy-start.3 = (f32[8,16,256]{2,1,0:T(8,128)}, f32[8,16,256]{2,1,0:T(8,128)S(1)}, u32[]{:S(2)}) copy-start(f32[8,16,256]{2,1,0:T(8,128)S(1)} %get-tuple-element.74) | copy-start | bytes 393220
  158.5 583.4 %all-reduce.7.cloned.1.call-start = ((), (), s32[]{:S(2)}) async-start(), calls=%async_computation.2 | async-start | bytes 262144 | tf_op jit(solution)/shard_map/psum | solution.py:56
  419.6 323.8 %copy-start.1 = (bf16[512,1024]{1,0:T(8,128)(2,1)S(1)}, bf16[512,1024]{1,0:T(8,128)(2,1)}, u32[]{:S(2)}) copy-start(bf16[512,1024]{1,0:T(8,128)(2,1)} %all-gather.4.cloned.1.call-done) | copy-start | bytes 3145732
  489.7 355.3 %all-gather.6.cloned.1.call-start = ((), (), s32[]{:S(2)}) async-start(), calls=%async_computation.5 | async-start | bytes 17301504 | tf_op jit(solution)/shard_map/all_gather | solution.py:65
  742.8 0.7 copy-start.2
  744.5 343.4 %all-reduce.9.cloned.1.call-start = ((), (), s32[]{:S(2)}) async-start(), calls=%async_computation.3 | async-start | bytes 262144 | tf_op jit(solution)/shard_map/psum | solution.py:78
  994.3 280.3 %all-reduce.11.cloned.1.call-start = ((), (), s32[]{:S(2)}) async-start(), calls=%async_computation.4 | async-start | bytes 262144 | tf_op jit(solution)/shard_map/psum | solution.py:78
Sparse Core Ops, SparseCore 0:
  10.5 64.1 all-gather.3
  158.6 247.4 all-reduce.4
  489.8 251.9 all-reduce.6
  744.7 100.2 all-gather.5
  994.4 93.5 all-reduce.8
  1179.3 95.2 all-reduce.10
